TPU v7x, 32 devices: a whole 2x2x4 slice. The times are simulated.
32 devices in a mesh: gx: 4 (over z), gy: 4 (over x, core), gz: 2 (over y).
Axes of the slice: x: 2, y: 2, z: 4, core: 2. Of those that a mesh axis runs over, the one named last changes fastest.
Arguments:
- right_sides: float32 [2, 32, 1024, 1024], P(None, ('gx', 'gy', 'gz')), may hold values from -6 to 6
- projector: float32 [2, 32, 1024, 192], P(None, ('gx', 'gy', 'gz')), may hold values from -0.1875 to 0.1875
- mixing: float32 [6, 2, 32, 2, 192, 192], P(None, None, ('gx', 'gy', 'gz')), may hold values from -0.3125 to 0.3125
- expander: float32 [64, 1024, 192], P(('gx', 'gy', 'gz')), may hold values from -0.4375 to 0.4375
Outputs:
- product: float32 [64, 1024, 1024], P(('gx', 'gy', 'gz'))
All inputs are finite; a program needn't handle non-finite values.
Results may differ from a plain program's by a relative error of at most 0.0001.
Values sent between devices are 32-bit elements; how exact they have to be, the bound alone decides.
A program may use at most 128 MiB of HBM per device.

v0:
```python
import functools

import jax
import jax.numpy as jnp
from jax import lax
from jax.experimental import pallas as pl
from jax.experimental.pallas import tpu as pltpu
from jax.sharding import PartitionSpec as P

AXES = ("gx", "gy", "gz")
CHUNKS = 4


def split(x):
    hi = x.astype(jnp.bfloat16)
    lo = (x - hi.astype(jnp.float32)).astype(jnp.bfloat16)
    return hi, lo


def product(a, b):
    dot = functools.partial(jnp.dot, preferred_element_type=jnp.float32)
    return dot(a[0], b[0]) + (dot(a[0], b[1]) + dot(a[1], b[0]))


def expand_kernel(e_ref, c_ref, o_ref):
    o_ref[0] = product(split(e_ref[0]), split(c_ref[0, 0]))


def expand(expander, coeffs):
    nodes, leaf, k = expander.shape
    chunks, _, _, width = coeffs.shape
    return pl.pallas_call(
        expand_kernel,
        grid=(nodes, chunks),
        in_specs=[
            pl.BlockSpec((1, leaf, k), lambda n, c: (n, 0, 0)),
            pl.BlockSpec((1, 1, k, width), lambda n, c: (c, n, 0, 0)),
        ],
        out_specs=pl.BlockSpec((1, leaf, width), lambda n, c: (n, 0, c)),
        out_shape=jax.ShapeDtypeStruct((nodes, leaf, chunks * width), jnp.float32),
    )(expander, coeffs)


def butterfly_kernel(sizes, x_ref, mix_ref, early, o_ref, *scratch):
    bits = sum(size.bit_length() - 1 for size in sizes)
    top = bits - 1
    arrived = scratch[:top]
    values = (x_ref,) + tuple(scratch[top : 2 * top])
    (
        swap_a, swap_b, paired, swap_c, final, landed,
        w_top, w_last, send, recv, w_send, w_recv,
    ) = scratch[2 * top :]
    chunks = x_ref.shape[0]
    coords = [lax.axis_index(name) for name in AXES]
    me = (coords[0] * sizes[1] + coords[1]) * sizes[2] + coords[2]

    def bit_of(b):
        return (me // (1 << b)) % 2

    def place(d):
        return {
            "gx": d // (sizes[1] * sizes[2]),
            "gy": (d // sizes[2]) % sizes[1],
            "gz": d % sizes[2],
        }

    flips = [me + (1 - 2 * bit_of(b)) * (1 << b) for b in range(bits)]
    first, last = bit_of(0), bit_of(top)
    ends = me + (last - first) - (last - first) * (1 << top)
    middle = first + last * (1 << top)
    for b in range(1, top):
        middle = middle + bit_of(b) * (1 << (top - b))
    ends_move = first != last
    middle_move = middle != me

    def remote(src, dst, sems, index, target):
        return pltpu.make_async_remote_copy(
            src_ref=src,
            dst_ref=dst,
            send_sem=sems[0].at[index],
            recv_sem=sems[1].at[index],
            device_id=place(target),
            device_id_type=pl.DeviceIdType.MESH,
        )

    def transfer(stage, c):
        index = (stage, c)
        sems = (send, recv)
        if stage < top:
            return remote(values[stage].at[c], arrived[stage].at[c], sems, index, flips[stage])
        if stage == top:
            return remote(
                values[top].at[c, 1 - first], swap_a.at[c, first], sems, index, flips[0]
            )
        if stage == top + 1:
            return remote(swap_a.at[c, 1 - last], swap_b.at[c, last], sems, index, flips[top])
        if stage == top + 2:
            return remote(paired.at[c, 1 - first], swap_c.at[c, first], sems, index, flips[0])
        return remote(final.at[c], landed.at[c], sems, index, middle)

    w_sems = (w_send, w_recv)
    moves_b = [
        remote(mix_ref.at[bits, n, s], w_last.at[n, s], w_sems, 2 * n + s, ends)
        for n in range(2)
        for s in range(2)
    ]
    move_c = remote(early.at[1 - last], w_top.at[last], w_sems, 4, flips[top])

    def mixed(weights, own, other, out):
        parts = [split(own[n]) for n in range(2)]
        others = parts[::-1] if other is None else [split(other[n]) for n in range(2)]
        for n in range(2):
            out[n] = product(split(weights[n, 0]), parts[n]) + product(
                split(weights[n, 1]), others[n]
            )

    barrier = pltpu.get_barrier_semaphore()
    for target in flips:
        pl.semaphore_signal(
            barrier, inc=1, device_id=place(target), device_id_type=pl.DeviceIdType.MESH
        )
    for moves, target in ((ends_move, ends), (middle_move, middle)):

        @pl.when(moves)
        def _():
            pl.semaphore_signal(
                barrier, inc=1, device_id=place(target), device_id_type=pl.DeviceIdType.MESH
            )

    moving = ends_move.astype(jnp.int32) + middle_move.astype(jnp.int32)
    pl.semaphore_wait(barrier, len(flips) + moving)

    def task(stage, c):
        if stage > 0:
            before = transfer(stage - 1, c)
            if stage - 1 == top + 3:
                pl.when(middle_move)(before.wait_recv)
            else:
                before.wait_recv()
        if 0 < stage <= top:
            mixed(
                mix_ref.at[stage - 1],
                values[stage - 1].at[c],
                arrived[stage - 1].at[c],
                values[stage].at[c],
            )
        if stage == top:
            swap_a[c, first] = values[top][c, first]
        if stage == top + 1:
            swap_b[c, last] = swap_a[c, last]
        if stage == top + 2:

            @pl.when(c == 0)
            def _():
                move_c.wait_recv()

            mixed(w_top, swap_b.at[c], None, paired.at[c])
            swap_c[c, first] = paired[c, first]
        if stage == top + 3:

            @pl.when((c == 0) & ends_move)
            def _():
                for move in moves_b:
                    move.wait_recv()

            mixed(w_last, swap_c.at[c], None, final.at[c])
            pl.when(middle_move)(transfer(stage, c).start)
        elif stage < top + 3:
            transfer(stage, c).start()
        else:

            @pl.when(middle_move)
            def _():
                o_ref[c] = landed[c]

            @pl.when(jnp.logical_not(middle_move))
            def _():
                o_ref[c] = final[c]

    w_top[last] = early[last]

    @pl.when(jnp.logical_not(ends_move))
    def _():
        w_last[...] = mix_ref[bits]

    stages = top + 5

    def step(t, carry):
        for stage in reversed(range(1, stages)):
            c = t - stage

            @pl.when((c >= 0) & (c < chunks))
            def _():
                task(stage, c)

        @pl.when(t + 1 < chunks)
        def _():
            task(0, t + 1)

        for i, move in enumerate(moves_b):
            pl.when((t == i) & ends_move)(move.start)

        return carry

    move_c.start()
    task(0, 0)
    lax.fori_loop(0, stages + chunks - 1, step, 0)

    def drain(c, carry):
        for stage in range(top + 3):
            transfer(stage, c).wait_send()
        pl.when(middle_move)(transfer(top + 3, c).wait_send)
        return carry

    lax.fori_loop(0, chunks, drain, 0)
    for move in moves_b:
        pl.when(ends_move)(move.wait_send)
    move_c.wait_send()


def butterfly(sizes, coeffs, mix, early):
    chunks, _, k, width = coeffs.shape
    top = sum(size.bit_length() - 1 for size in sizes) - 1
    block = pltpu.VMEM(coeffs.shape, jnp.float32)
    weight = pltpu.VMEM((2, 2, k, k), jnp.float32)
    sems = pltpu.SemaphoreType.DMA((top + 4, chunks))
    w_sems = pltpu.SemaphoreType.DMA((5,))
    return pl.pallas_call(
        functools.partial(butterfly_kernel, sizes),
        out_shape=jax.ShapeDtypeStruct(coeffs.shape, jnp.float32),
        in_specs=[pl.BlockSpec(memory_space=pltpu.VMEM)] * 3,
        out_specs=pl.BlockSpec(memory_space=pltpu.VMEM),
        scratch_shapes=[block] * (2 * top + 6) + [weight] * 2 + [sems, sems, w_sems, w_sems],
        compiler_params=pltpu.CompilerParams(
            collective_id=0, has_side_effects=True, vmem_limit_bytes=60 * 2**20
        ),
    )(coeffs, mix, early)


def shards(right_sides, projector, mixing, expander):
    data = right_sides[:, 0]
    proj = projector[:, 0]
    mix = mixing[:, :, 0]
    sizes = tuple(lax.axis_size(name) for name in AXES)
    width = data.shape[2] // CHUNKS
    coeffs = jnp.stack(
        [
            jnp.einsum(
                "nlk,nlr->nkr",
                proj,
                data[:, :, i * width : (i + 1) * width],
                precision=lax.Precision.HIGHEST,
            )
            for i in range(CHUNKS)
        ]
    )
    total = lax.axis_size(AXES)
    outer = mix[mix.shape[0] - 2]
    own_zero = lax.axis_index(AXES) % 2 == 0
    arrived = lax.ppermute(
        jnp.where(own_zero, outer[1], outer[0]), AXES, [(d, d ^ 1) for d in range(total)]
    )
    early = jnp.stack(
        [jnp.where(own_zero, outer[0], arrived), jnp.where(own_zero, arrived, outer[1])]
    )
    return expand(expander, butterfly(sizes, coeffs, mix, early))


def solution(mesh):
    placed = (
        P(None, AXES, None, None),
        P(None, AXES, None, None),
        P(None, None, AXES, None, None, None),
        P(AXES, None, None),
    )
    return jax.shard_map(
        shards, mesh=mesh, in_specs=placed, out_specs=P(AXES, None, None), check_vma=False
    )
```

profile of v0, /device:TPU:1, one launch (start us, length us, event | category | flops | bytes accessed | tf_op | source)
XLA Modules:
  0.0 167.4 jit_solution(14506604524042464689)
XLA Ops:
  0.0 0.0 copy-start
  0.0 2.0 %bitcast_select_fusion.1 = f32[2,192,192]{2,1,0:T(8,128)} fusion(f32[6,2,1,2,192,192]{5,4,3,2,1,0:T(8,128)} %param.6, pred[]{:T(512)S(6)} %eq.5), kind=kLoop, calls=%fused_computation.19 | loop fusion | flops 73728 | bytes 884737 | tf_op jit(solution)/shard_map/jit(_where)/select_n | solution.py:261
  2.0 2.1 %collective-permute-start = (f32[2,192,192]{2,1,0:T(8,128)}, f32[2,192,192]{2,1,0:T(8,128)}, u32[]{:S(2)}, u32[]{:S(2)}) collective-permute-start(f32[2,192,192]{2,1,0:T(8,128)} %bitcast_select_fusion.1), channel_id=1, source_target_pairs={{0,1},{1,0},{2,3},{3,2},{4,5},{5,4},{6,7},{7,6},{8,9},{9,8},{10,11... | collective-permute-start | bytes 884744 | tf_op jit(solution)/shard_map/ppermute | solution.py:260
  4.1 0.0 copy-done
  4.1 3.3 %fusion.27 = f32[1,2,192,256]{3,2,1,0:T(8,128)S(1)} fusion(f32[2,1024,1024]{2,1,0:T(8,128)} %bitcast.42, f32[2,1,1024,192]{2,3,1,0:T(8,128)S(1)} %copy-done), kind=kOutput, calls=%fused_computation.16 | convolution fusion | flops 1207959552 | bytes 4063232 | tf_op jit(solution)/shard_map/nlk,nlr->nkr/dot_general | solution.py:248
  7.4 4.0 %fusion.22 = f32[1,2,192,256]{3,2,1,0:T(8,128)} fusion(f32[2,1024,1024]{2,1,0:T(8,128)} %bitcast.43, f32[2,1,1024,192]{2,3,1,0:T(8,128)S(1)} %copy-done), kind=kOutput, calls=%fused_computation.15 | convolution fusion | flops 1207959552 | bytes 4063232 | tf_op jit(solution)/shard_map/nlk,nlr->nkr/dot_general | solution.py:248
  11.4 0.0 copy-start.1
  11.4 4.2 %fusion.17 = f32[1,2,192,256]{3,2,1,0:T(8,128)} fusion(f32[2,1024,1024]{2,1,0:T(8,128)} %bitcast.44, f32[2,1,1024,192]{2,3,1,0:T(8,128)S(1)} %copy-done), kind=kOutput, calls=%fused_computation.14 | convolution fusion | flops 1207959552 | bytes 4063232 | tf_op jit(solution)/shard_map/nlk,nlr->nkr/dot_general | solution.py:248
  15.5 0.0 copy-done.1
  15.5 1.8 %copy.5.e_ref = f32[2,1024,192]{2,1,0:T(8,128)} copy(f32[2,1024,192]{1,2,0:T(8,128)S(1)} %copy-done.1) | data formatting | bytes 3145728 | tf_op args[3]
  17.4 0.0 copy-start.2
  17.4 0.0 copy-start.3
  17.4 3.3 %fusion.12 = f32[1,2,192,256]{3,2,1,0:T(8,128)S(1)} fusion(f32[2,1024,1024]{2,1,0:T(8,128)} %bitcast.45, f32[2,1,1024,192]{2,3,1,0:T(8,128)S(1)} %copy-done), kind=kOutput, calls=%fused_computation.13 | convolution fusion | flops 1207959552 | bytes 4063232 | tf_op jit(solution)/shard_map/nlk,nlr->nkr/dot_general | solution.py:248
  20.7 0.0 copy-done.2
  20.7 0.0 copy-done.3
  20.7 1.3 pad_maximum_fusion.x_ref
  22.0 0.0 collective-permute-done
  22.0 1.3 fusion.33
  23.3 0.9 pad_maximum_fusion.1.early
  24.2 133.8 %shard_map.46.c_ref = f32[4,2,192,256]{3,2,1,0:T(8,128)} custom-call(f32[4,2,192,256]{3,2,1,0:T(8,128)} %pad_maximum_fusion.x_ref, f32[6,2,2,192,192]{4,3,2,1,0:T(8,128)} %bitcast.41, f32[2,2,192,192]{3,2,1,0:T(8,128)} %pad_maximum_fusion.1.early), custom_call_target="tpu_custom_call" | custom-call | tf_op jit(solution)/shard_map/pallas_call | solution.py:228
  158.1 9.3 %shard_map.47 = f32[2,1024,1024]{2,1,0:T(8,128)} custom-call(f32[2,1024,192]{2,1,0:T(8,128)} %copy.5.e_ref, f32[4,2,192,256]{3,2,1,0:T(8,128)} %shard_map.46.c_ref), custom_call_target="tpu_custom_call" | custom-call | tf_op jit(solution)/shard_map/pallas_call | solution.py:32
Async XLA Ops:
  0.0 4.1 %copy-start = (f32[2,1,1024,192]{2,3,1,0:T(8,128)S(1)}, f32[2,1,1024,192]{2,3,1,0:T(8,128)}, u32[]{:S(2)}) copy-start(f32[2,1,1024,192]{2,3,1,0:T(8,128)} %param.5) | copy-start | bytes 4718596
  2.0 20.0 %collective-permute-start = (f32[2,192,192]{2,1,0:T(8,128)}, f32[2,192,192]{2,1,0:T(8,128)}, u32[]{:S(2)}, u32[]{:S(2)}) collective-permute-start(f32[2,192,192]{2,1,0:T(8,128)} %bitcast_select_fusion.1), channel_id=1, source_target_pairs={{0,1},{1,0},{2,3},{3,2},{4,5},{5,4},{6,7},{7,6},{8,9},{9,8},{10,11... | collective-permute-start | bytes 884744 | tf_op jit(solution)/shard_map/ppermute | solution.py:260
  11.4 4.2 %copy-start.1 = (f32[2,1024,192]{1,2,0:T(8,128)S(1)}, f32[2,1024,192]{1,2,0:T(8,128)}, u32[]{:S(2)}) copy-start(f32[2,1024,192]{1,2,0:T(8,128)} %param.7) | copy-start | bytes 4718596
  17.4 3.4 %copy-start.2 = (f32[1,2,192,256]{3,2,1,0:T(8,128)S(1)}, f32[1,2,192,256]{3,2,1,0:T(8,128)}, u32[]{:S(2)}) copy-start(f32[1,2,192,256]{3,2,1,0:T(8,128)} %fusion.22) | copy-start | bytes 1179652
  17.4 3.4 %copy-start.3 = (f32[1,2,192,256]{3,2,1,0:T(8,128)S(1)}, f32[1,2,192,256]{3,2,1,0:T(8,128)}, u32[]{:S(2)}) copy-start(f32[1,2,192,256]{3,2,1,0:T(8,128)} %fusion.17) | copy-start | bytes 1179652
where the time goes:
time: 168 us; the launch traced here: 167 us
  Pallas kernels  143 us (85%)
  matrix products  14.8 us (9%)
  other arithmetic  5.51 us (3%)
  starting transfers between devices  2.06 us (1%)
  local copies, waits for them, and re-layouts  1.84 us (1%)
    pallas_call x1, Pallas kernels, butterfly(): pl.pallas_call(functools.partial(butterfly_kernel, sizes), out_shape=jax....  134 us
    dot_general x4, matrix products, shards(): jnp.einsum('nlk,nlr->nkr', proj, data[:, :, i * width:(i + 1) * width], p...  14.8 us
    pallas_call x1, Pallas kernels, expand(): pl.pallas_call(expand_kernel, grid=(nodes, chunks), in_specs=[pl.BlockSpe...  9.32 us
  transfers between devices with their start and end apart: 1, of which 0 were waited for; matrix products, arithmetic and copies ran while one was open for 11% of the time, Pallas kernels for 0%

commit v1 on v0

v1 whole, which is shorter than its diff:
```python
import functools

import jax
import jax.numpy as jnp
from jax import lax
from jax.experimental import pallas as pl
from jax.experimental.pallas import tpu as pltpu
from jax.sharding import PartitionSpec as P

AXES = ("gx", "gy", "gz")
CHUNKS = 8
BLOCKS = 4
ORDER = (
    15, 0, 10, 0, 13, 0, 12, 11, 21, 1, 2, 1, 14, 1, 2, 0, 0, 3, 0, 3, 4, 20, 2, 1, 2, 1, 3, 5, 2, 0, 4, 1, 3, 6, 5, 4,
    5, 3, 2, 1, 0, 4, 6, 2, 4, 6, 5, 5, 3, 7, 1, 6, 2, 7, 3, 4, 6, 5, 7, 4, 3, 8, 6, 5, 7, 8, 4, 6, 5, 7, 7, 6, 8, 8,
    7, 8, 8, 7, 8, 8,
)


def split(x):
    hi = x.astype(jnp.bfloat16)
    lo = (x - hi.astype(jnp.float32)).astype(jnp.bfloat16)
    return hi, lo


def product(a, b):
    dot = functools.partial(jnp.dot, preferred_element_type=jnp.float32)
    return dot(a[0], b[0]) + (dot(a[0], b[1]) + dot(a[1], b[0]))


def expand_kernel(e_ref, c_ref, o_ref):
    o_ref[0] = product(split(e_ref[0]), split(c_ref[0]))


def expand(expander, coeffs):
    nodes, leaf, k = expander.shape
    rhs = coeffs.shape[2]
    width = rhs // BLOCKS
    return pl.pallas_call(
        expand_kernel,
        grid=(nodes, BLOCKS),
        in_specs=[
            pl.BlockSpec((1, leaf, k), lambda n, c: (n, 0, 0)),
            pl.BlockSpec((1, k, width), lambda n, c: (n, 0, c)),
        ],
        out_specs=pl.BlockSpec((1, leaf, width), lambda n, c: (n, 0, c)),
        out_shape=jax.ShapeDtypeStruct((nodes, leaf, rhs), jnp.float32),
    )(expander, coeffs)


def plan(bits):
    slots, local = list(range(bits)), bits
    steps, places = [], {}

    def swap(slot, level):
        nonlocal local
        slots[slot], local = local, slots[slot]
        steps.append((slot, False, level))
        if level is not None:
            places[level] = (tuple(slots), local)

    def show(slot):
        steps.append((slot, True, slot))
        places[slot] = (tuple(slots), local)

    half = bits // 2
    show(0)
    for k in range(1, half):
        swap(k, k)
    if bits % 2:
        show(half)
    for k in reversed(range(1, half)):
        swap(bits - 1 - k, bits - 1 - k)
        swap(k, None)
    swap(0, None)
    ahead = (tuple(slots), local)
    swap(bits - 1, bits - 1)
    swap(0, bits)
    return steps, places, ahead


def order(bits, count, chunks):
    tasks = list(ORDER)
    whole = [tasks.count(s) == chunks for s in range(count + 1)] + [tasks.count(10 + i) for i in range(bits + 1)]
    if not all(whole) or len(tasks) != (count + 1) * chunks + bits + 3:
        timed = [(3 * c + 4 * s, s) for c in range(chunks) for s in range(count + 1)]
        timed += [(l - bits, 100 + l) for l in range(bits + 1)] + [(0, 200), (0, 201)]
        tasks = [task for _, task in sorted(timed)]
    else:
        tasks = [task if task < 10 else 90 + task if task < 20 else 180 + task for task in tasks]
    ticks, at = [[]], -count - 1
    for task in tasks:
        rank = task if task >= 100 else -task
        if rank <= at:
            ticks.append([])
        ticks[-1].append(task)
        at = rank
    return ticks


def butterfly_kernel(sizes, x_hbm, p_hbm, mix_hbm, o_ref, *scratch):
    bits = sum(size.bit_length() - 1 for size in sizes)
    levels = bits + 1
    steps, places, ahead = plan(bits)
    count = len(steps)
    values, arrived = scratch[:count], scratch[count : 2 * count]
    (
        xbuf, pbuf, p_hi, p_lo, mixes, packed, weights, early, relay, w_hi, w_lo,
        x_sem, p_sem, mix_sem, send, recv, w_send, w_recv,
    ) = scratch[2 * count :]
    chunks, _, k, width = values[0].shape
    part = k // 2
    coords = [lax.axis_index(name) for name in AXES]
    me = (coords[0] * sizes[1] + coords[1]) * sizes[2] + coords[2]

    def bit_of(device, b):
        return (device // (1 << b)) % 2

    def flip(device, b):
        return device + (1 - 2 * bit_of(device, b)) * (1 << b)

    def place(d):
        return {
            "gx": d // (sizes[1] * sizes[2]),
            "gy": (d // sizes[2]) % sizes[1],
            "gz": d % sizes[2],
        }

    mine = [bit_of(me, b) for b in range(bits)]

    def goes(layout, c):
        slots, local = layout
        of_node = mine + [c]
        return sum(of_node[slot] * (1 << b) for b, slot in enumerate(slots)), of_node[local]

    def comes(layout, index):
        slots, local = layout
        of_node = [None] * (bits + 1)
        for b, slot in enumerate(slots):
            of_node[slot] = mine[b]
        of_node[local] = index
        return sum(of_node[b] * (1 << b) for b in range(bits))

    def reverse(device):
        return sum(bit_of(device, b) * (1 << (bits - 1 - b)) for b in range(bits))

    def remote(src, dst, s_sem, r_sem, target):
        return pltpu.make_async_remote_copy(
            src_ref=src,
            dst_ref=dst,
            send_sem=s_sem,
            recv_sem=r_sem,
            device_id=place(target),
            device_id_type=pl.DeviceIdType.MESH,
        )

    def transfer(s, c):
        slot, full, _ = steps[s]
        src = values[s].at[c] if full else values[s].at[c, 1 - mine[slot]]
        return remote(src, arrived[s].at[c], send.at[s, c], recv.at[s, c], flip(me, slot))

    def straight(level, c):
        target, index = goes(ahead if level == bits - 1 else places[level], c)
        there = early if level == bits - 1 else weights.at[level]
        copy = remote(
            packed.at[level, c], there.at[index],
            w_send.at[level, c], w_recv.at[level, index], target,
        )
        return copy, target, index

    last = bits - 1
    hop = remote(
        early.at[1 - mine[last]], weights.at[last, mine[last]],
        w_send.at[bits + 1, 0], w_recv.at[bits + 1, 0], flip(me, last),
    )
    home = reverse(me)
    apart = mine[0] != mine[last]
    lower, upper = pl.ds(0, part), pl.ds(part, part)
    direct = remote(
        packed.at[bits, :, lower], weights.at[bits, :, lower],
        w_send.at[bits, 0], w_recv.at[bits, 0], home,
    )
    beside = remote(
        packed.at[bits, :, upper], weights.at[bits, :, upper],
        w_send.at[bits, 1], w_recv.at[bits, 1], home,
    )
    around = remote(
        packed.at[bits, :, upper], relay, w_send.at[bits, 1], w_recv.at[bits + 1, 1], flip(me, 0)
    )
    onward = remote(
        relay, weights.at[bits, :, upper],
        w_send.at[bits + 1, 1], w_recv.at[bits, 1], reverse(flip(me, 0)),
    )

    def when(condition, action):
        pl.when(condition)(action)

    def greet(target):
        pl.semaphore_signal(
            barrier, inc=1, device_id=place(target), device_id_type=pl.DeviceIdType.MESH
        )

    barrier = pltpu.get_barrier_semaphore()
    greeted = jnp.int32(bits)
    for b in range(bits):
        greet(flip(me, b))
    layouts = [places[level] for level in range(1, last)] + [ahead]
    for layout in layouts:
        for c in range(2):
            source = comes(layout, c)
            when(source != me, functools.partial(greet, source))
            greeted = greeted + (goes(layout, c)[0] != me).astype(jnp.int32)
    when(home != me, functools.partial(greet, home))
    greeted = greeted + (home != me).astype(jnp.int32)
    when(apart, functools.partial(greet, flip(home, 0)))
    greeted = greeted + jnp.logical_not(apart).astype(jnp.int32)

    def load_x(c):
        return pltpu.make_async_copy(
            x_hbm.at[:, :, pl.ds(pl.multiple_of(c * width, width), width)],
            xbuf.at[c % 2], x_sem.at[c % 2],
        )

    load_p = pltpu.make_async_copy(p_hbm, pbuf, p_sem)

    def load_mix(level):
        return pltpu.make_async_copy(mix_hbm.at[level], mixes.at[level], mix_sem.at[level])

    load_mix(0).start()
    load_p.start()
    load_x(0).start()
    load_x(1).start()
    for level in range(1, levels):
        load_mix(level).start()

    def send_weights(level):
        load_mix(level).wait()
        for c in range(2):
            packed[level, c] = jnp.concatenate([mixes[level, c, 0], mixes[level, c, 1]], axis=1)
        if level == 0:
            weights[0] = packed[0]
        elif level < bits:
            there = early if level == last else weights.at[level]
            for c in range(2):
                copy, target, index = straight(level, c)

                @pl.when(target != me)
                def _():
                    copy.start()

                @pl.when(target == me)
                def _():
                    there[index] = packed[level, c]
        else:

            @pl.when(home != me)
            def _():
                direct.start()

            @pl.when(home == me)
            def _():
                weights[bits] = packed[bits]

            @pl.when(apart)
            def _():
                around.start()

            @pl.when(jnp.logical_not(apart) & (home != me))
            def _():
                beside.start()

    def forward_last():
        for index in range(2):

            @pl.when(comes(ahead, index) != me)
            def _():
                remote(
                    packed.at[last, 0], early.at[index],
                    w_send.at[last, 0], w_recv.at[last, index], me,
                ).wait_recv()

        weights[last, mine[last]] = early[mine[last]]
        hop.start()

    def forward_relay():
        @pl.when(jnp.logical_not(apart))
        def _():
            around.wait_recv()
            onward.start()

    def take_weights(level):
        if level == 0:
            pass
        elif level < last:
            for index in range(2):

                @pl.when(comes(places[level], index) != me)
                def _():
                    remote(
                        packed.at[level, 0], weights.at[level, index],
                        w_send.at[level, 0], w_recv.at[level, index], me,
                    ).wait_recv()
        elif level == last:
            hop.wait_recv()
        else:

            @pl.when(home != me)
            def _():
                direct.wait_recv()
                beside.wait_recv()

        for index in range(2):
            w_hi[level, index], w_lo[level, index] = split(weights[level, index])

    def mixed(level, index, one, other):
        pair = [jnp.concatenate([a, b], axis=0) for a, b in zip(one, other)]
        return product((w_hi[level, index], w_lo[level, index]), pair)

    def task(s, c):
        if s == 0:
            load_x(c).wait()
            for n in range(2):
                values[0][c, n] = product((p_hi[n], p_lo[n]), split(xbuf[c % 2, n]))
            pl.when(c + 2 < chunks)(lambda: load_x(c + 2).start())
        else:
            slot, full, level = steps[s - 1]
            bit = mine[slot]
            columns = pl.ds(pl.multiple_of(c * width, width), width)
            out = o_ref.at[:, :, columns] if s == count else values[s].at[c]
            if level is not None:
                pl.when(c == 0)(lambda: take_weights(level))
            transfer(s - 1, c).wait_recv()
            own, other = values[s - 1].at[c], arrived[s - 1].at[c]
            if full:
                for n in range(2):
                    out[n] = mixed(level, n, split(own[n]), split(other[n]))
            elif level is None:
                out[bit] = own[bit]
                out[1 - bit] = other[...]
            else:
                a, b = split(own[bit]), split(other[...])
                out[bit] = mixed(level, bit, a, b)
                out[1 - bit] = mixed(level, 1 - bit, b, a)
        if s < count:
            transfer(s, c).start()

    timetable = order(bits, count, chunks)

    def due(t, task):
        words = [0] * (len(timetable) // 31 + 1)
        for i, tasks in enumerate(timetable):
            words[i // 31] |= (task in tasks) << (i % 31)
        word = jnp.int32(words[0])
        for i, other in enumerate(words[1:]):
            word = jnp.where(t >= 31 * (i + 1), other, word)
        return lax.shift_right_logical(word, t % 31) % 2

    def tick(t, carry):
        done = list(carry)
        for s in reversed(range(count + 1)):
            now = due(t, s)
            pl.when(now == 1)(functools.partial(task, s, done[s]))
            done[s] = done[s] + now
        for level in range(levels):
            pl.when(due(t, 100 + level) == 1)(functools.partial(send_weights, level))
        pl.when(due(t, 200) == 1)(forward_last)
        pl.when(due(t, 201) == 1)(forward_relay)
        return tuple(done)

    pl.semaphore_wait(barrier, greeted)
    load_p.wait()
    for n in range(2):
        p_hi[n], p_lo[n] = split(pbuf[n])
    lax.fori_loop(0, len(timetable), tick, (jnp.int32(0),) * (count + 1))

    def drain(c, carry):
        for s in range(count):
            transfer(s, c).wait_send()
        return carry

    lax.fori_loop(0, chunks, drain, 0)
    for level in range(1, bits):
        for c in range(2):
            copy, target, _ = straight(level, c)
            pl.when(target != me)(copy.wait_send)
    hop.wait_send()
    pl.when(home != me)(direct.wait_send)
    pl.when(apart)(around.wait_send)
    pl.when(jnp.logical_not(apart) & (home != me))(beside.wait_send)
    pl.when(jnp.logical_not(apart))(onward.wait_send)


def butterfly(sizes, data, proj, mix):
    _, leaf, rhs = data.shape
    k = proj.shape[1]
    levels = mix.shape[0]
    bits = levels - 1
    width = rhs // CHUNKS
    steps, _, _ = plan(bits)
    f32, bf16 = jnp.float32, jnp.bfloat16
    held = [pltpu.VMEM((CHUNKS, 2, k, width), f32) for _ in steps]
    landed = [pltpu.VMEM((CHUNKS,) + ((2,) if full else ()) + (k, width), f32) for _, full, _ in steps]
    dma = pltpu.SemaphoreType.DMA
    return pl.pallas_call(
        functools.partial(butterfly_kernel, sizes),
        out_shape=jax.ShapeDtypeStruct((2, k, rhs), f32),
        in_specs=[pl.BlockSpec(memory_space=pl.ANY)] * 3,
        out_specs=pl.BlockSpec(memory_space=pltpu.VMEM),
        scratch_shapes=held + landed + [
            pltpu.VMEM((2, 2, leaf, width), f32),
            pltpu.VMEM((2, k, leaf), f32),
            pltpu.VMEM((2, k, leaf), bf16),
            pltpu.VMEM((2, k, leaf), bf16),
            pltpu.VMEM((levels, 2, 2, k, k), f32),
            pltpu.VMEM((levels, 2, k, 2 * k), f32),
            pltpu.VMEM((levels, 2, k, 2 * k), f32),
            pltpu.VMEM((2, k, 2 * k), f32),
            pltpu.VMEM((2, k // 2, 2 * k), f32),
            pltpu.VMEM((levels, 2, k, 2 * k), bf16),
            pltpu.VMEM((levels, 2, k, 2 * k), bf16),
            dma((2,)),
            dma,
            dma((levels,)),
            dma((len(steps), CHUNKS)),
            dma((len(steps), CHUNKS)),
            dma((levels + 1, 2)),
            dma((levels + 1, 2)),
        ],
        compiler_params=pltpu.CompilerParams(
            collective_id=0, has_side_effects=True, vmem_limit_bytes=60 * 2**20
        ),
    )(data, proj, mix)


def shards(right_sides, projector, mixing, expander):
    sizes = tuple(lax.axis_size(name) for name in AXES)
    proj = jnp.swapaxes(projector[:, 0], 1, 2)
    return expand(expander, butterfly(sizes, right_sides[:, 0], proj, mixing[:, :, 0]))


def solution(mesh):
    placed = (
        P(None, AXES, None, None),
        P(None, AXES, None, None),
        P(None, None, AXES, None, None, None),
        P(AXES, None, None),
    )
    return jax.shard_map(
        shards, mesh=mesh, in_specs=placed, out_specs=P(AXES, None, None), check_vma=False
    )
```

time: 168 us -> 110 us (0.65)
  Pallas kernels: 143 us -> 106 us
  matrix products: 14.8 us -> 0 us
  other arithmetic: 5.51 us -> 0 us
  starting transfers between devices: 2.06 us -> 0 us
    pallas_call x1, Pallas kernels: 134 us -> 97 us  [butterfly(): pl.pallas_call(functools.partial(butterfly_kernel, sizes), out_shape=jax....]
    dot_general x4 -> x0, matrix products: 14.8 us -> none  [shards(): jnp.einsum('nlk,nlr->nkr', proj, data[:, :, i * width:(i + 1) * width], p...]
    another operation x3 -> x0, other arithmetic: 3.49 us -> none  [the longest x2 2.24 us: shards(): jnp.stack([jnp.where(own_zero, outer[0], arrived), jnp.where(own_zero, ar...]
    ppermute x1 -> x0, starting transfers between devices: 2.06 us -> none  [shards(): lax.ppermute(jnp.where(own_zero, outer[1], outer[0]), AXES, [(d, d ^ 1) f...]
    select_n x1 -> x0, other arithmetic: 2.02 us -> none  [shards(): jnp.where(own_zero, outer[1], outer[0])]
  transfers between devices with their start and end apart: 1 -> 0, of which waited for: 0 -> 0; matrix products, arithmetic and copies ran while one was open for 11% -> 0% of each run, Pallas kernels for 0% -> 0%
where the time goes in v1:
time: 110 us; the launch traced here: 108 us
  Pallas kernels  106 us (96%)
  local copies, waits for them, and re-layouts  1.85 us (2%)
    pallas_call x1, Pallas kernels, butterfly(): pl.pallas_call(functools.partial(butterfly_kernel, sizes), out_shape=jax....  97 us
    pallas_call x1, Pallas kernels, expand(): pl.pallas_call(expand_kernel, grid=(nodes, BLOCKS), in_specs=[pl.BlockSpe...  9.41 us

profile of v1, /device:TPU:1, one launch (start us, length us, event | category | flops | bytes accessed | tf_op | source)
XLA Modules:
  0.0 108.2 jit_solution(5473475477104418511)
XLA Ops:
  0.0 0.0 copy-start
  0.0 97.0 %shard_map.46.c_ref = f32[2,192,1024]{2,1,0:T(8,128)} custom-call(f32[2,1024,1024]{2,1,0:T(8,128)} %bitcast.5, f32[2,192,1024]{2,1,0:T(8,128)} %bitcast.7, f32[6,2,2,192,192]{4,3,2,1,0:T(8,128)} %bitcast.6), custom_call_target="tpu_custom_call" | custom-call | tf_op jit(solution)/shard_map/pallas_call | solution.py:404
  97.0 0.0 copy-done
  97.0 1.8 %copy.5.e_ref = f32[2,1024,192]{2,1,0:T(8,128)} copy(f32[2,1024,192]{1,2,0:T(8,128)S(1)} %copy-done) | data formatting | bytes 3145728 | tf_op args[3]
  98.8 9.4 %shard_map.47 = f32[2,1024,1024]{2,1,0:T(8,128)} custom-call(f32[2,1024,192]{2,1,0:T(8,128)} %copy.5.e_ref, f32[2,192,1024]{2,1,0:T(8,128)} %shard_map.46.c_ref), custom_call_target="tpu_custom_call" | custom-call | tf_op jit(solution)/shard_map/pallas_call | solution.py:39
Async XLA Ops:
  0.0 97.0 %copy-start = (f32[2,1024,192]{1,2,0:T(8,128)S(1)}, f32[2,1024,192]{1,2,0:T(8,128)}, u32[]{:S(2)}) copy-start(f32[2,1024,192]{1,2,0:T(8,128)} %param.7) | copy-start | bytes 4718596

commit v2 on v1

--- a/solution.py
+++ b/solution.py
@@ -9,7 +9,6 @@
 
 AXES = ("gx", "gy", "gz")
 CHUNKS = 8
-BLOCKS = 4
 ORDER = (
     15, 0, 10, 0, 13, 0, 12, 11, 21, 1, 2, 1, 14, 1, 2, 0, 0, 3, 0, 3, 4, 20, 2, 1, 2, 1, 3, 5, 2, 0, 4, 1, 3, 6, 5, 4,
     5, 3, 2, 1, 0, 4, 6, 2, 4, 6, 5, 5, 3, 7, 1, 6, 2, 7, 3, 4, 6, 5, 7, 4, 3, 8, 6, 5, 7, 8, 4, 6, 5, 7, 7, 6, 8, 8,
@@ -23,28 +22,30 @@
     return hi, lo
 
 
-def product(a, b):
-    dot = functools.partial(jnp.dot, preferred_element_type=jnp.float32)
+def product(a, b, over=((1,), (0,))):
+    def dot(x, y):
+        return lax.dot_general(x, y, (over, ((), ())), preferred_element_type=jnp.float32)
+
     return dot(a[0], b[0]) + (dot(a[0], b[1]) + dot(a[1], b[0]))
 
 
 def expand_kernel(e_ref, c_ref, o_ref):
-    o_ref[0] = product(split(e_ref[0]), split(c_ref[0]))
+    o_ref[0] = product(split(e_ref[0]), split(c_ref[0]), ((0,), (0,)))
 
 
 def expand(expander, coeffs):
-    nodes, leaf, k = expander.shape
+    nodes, k, leaf = expander.shape
     rhs = coeffs.shape[2]
-    width = rhs // BLOCKS
     return pl.pallas_call(
         expand_kernel,
-        grid=(nodes, BLOCKS),
+        grid=(nodes,),
         in_specs=[
-            pl.BlockSpec((1, leaf, k), lambda n, c: (n, 0, 0)),
-            pl.BlockSpec((1, k, width), lambda n, c: (n, 0, c)),
+            pl.BlockSpec((1, k, leaf), lambda n: (n, 0, 0)),
+            pl.BlockSpec((1, k, rhs), lambda n: (n, 0, 0)),
         ],
-        out_specs=pl.BlockSpec((1, leaf, width), lambda n, c: (n, 0, c)),
+        out_specs=pl.BlockSpec((1, leaf, rhs), lambda n: (n, 0, 0)),
         out_shape=jax.ShapeDtypeStruct((nodes, leaf, rhs), jnp.float32),
+        compiler_params=pltpu.CompilerParams(vmem_limit_bytes=32 * 2**20),
     )(expander, coeffs)
 
 
@@ -226,12 +227,12 @@
     def load_mix(level):
         return pltpu.make_async_copy(mix_hbm.at[level], mixes.at[level], mix_sem.at[level])
 
-    load_mix(0).start()
+    load_mix(bits).start()
     load_p.start()
     load_x(0).start()
+    for level in range(bits):
+        load_mix(level).start()
     load_x(1).start()
-    for level in range(1, levels):
-        load_mix(level).start()
 
     def send_weights(level):
         load_mix(level).wait()
@@ -318,6 +319,13 @@
 
     def task(s, c):
         if s == 0:
+
+            @pl.when(c == 0)
+            def _():
+                load_p.wait()
+                for n in range(2):
+                    p_hi[n], p_lo[n] = split(pbuf[n])
+
             load_x(c).wait()
             for n in range(2):
                 values[0][c, n] = product((p_hi[n], p_lo[n]), split(xbuf[c % 2, n]))
@@ -346,10 +354,10 @@
 
     timetable = order(bits, count, chunks)
 
-    def due(t, task):
+    def due(t, *kinds):
         words = [0] * (len(timetable) // 31 + 1)
         for i, tasks in enumerate(timetable):
-            words[i // 31] |= (task in tasks) << (i % 31)
+            words[i // 31] |= any(kind in tasks for kind in kinds) << (i % 31)
         word = jnp.int32(words[0])
         for i, other in enumerate(words[1:]):
             word = jnp.where(t >= 31 * (i + 1), other, word)
@@ -361,16 +369,17 @@
             now = due(t, s)
             pl.when(now == 1)(functools.partial(task, s, done[s]))
             done[s] = done[s] + now
-        for level in range(levels):
-            pl.when(due(t, 100 + level) == 1)(functools.partial(send_weights, level))
-        pl.when(due(t, 200) == 1)(forward_last)
-        pl.when(due(t, 201) == 1)(forward_relay)
+        others = [(100 + level, functools.partial(send_weights, level)) for level in range(levels)]
+        others += [(200, forward_last), (201, forward_relay)]
+
+        @pl.when(due(t, *(kind for kind, _ in others)) == 1)
+        def _():
+            for kind, action in others:
+                pl.when(due(t, kind) == 1)(action)
+
         return tuple(done)
 
     pl.semaphore_wait(barrier, greeted)
-    load_p.wait()
-    for n in range(2):
-        p_hi[n], p_lo[n] = split(pbuf[n])
     lax.fori_loop(0, len(timetable), tick, (jnp.int32(0),) * (count + 1))
 
     def drain(c, carry):
@@ -404,7 +413,7 @@
     return pl.pallas_call(
         functools.partial(butterfly_kernel, sizes),
         out_shape=jax.ShapeDtypeStruct((2, k, rhs), f32),
-        in_specs=[pl.BlockSpec(memory_space=pl.ANY)] * 3,
+        in_specs=[pl.BlockSpec(memory_space=pltpu.HBM)] * 3,
         out_specs=pl.BlockSpec(memory_space=pltpu.VMEM),
         scratch_shapes=held + landed + [
             pltpu.VMEM((2, 2, leaf, width), f32),
@@ -427,7 +436,7 @@
             dma((levels + 1, 2)),
         ],
         compiler_params=pltpu.CompilerParams(
-            collective_id=0, has_side_effects=True, vmem_limit_bytes=60 * 2**20
+            collective_id=0, has_side_effects=True, vmem_limit_bytes=(46 + levels) * 2**20
         ),
     )(data, proj, mix)
 
@@ -435,7 +444,7 @@
 def shards(right_sides, projector, mixing, expander):
     sizes = tuple(lax.axis_size(name) for name in AXES)
     proj = jnp.swapaxes(projector[:, 0], 1, 2)
-    return expand(expander, butterfly(sizes, right_sides[:, 0], proj, mixing[:, :, 0]))
+    return expand(jnp.swapaxes(expander, 1, 2), butterfly(sizes, right_sides[:, 0], proj, mixing[:, :, 0]))
 
 
 def solution(mesh):

time: 110 us -> 103 us (0.936)
  Pallas kernels: 106 us -> 101 us
  local copies, waits for them, and re-layouts: 1.85 us -> 0.01 us
    pallas_call x1, Pallas kernels: 9.41 us -> 5.75 us  [expand(): pl.pallas_call(expand_kernel, grid=(nodes,), in_specs=[pl.BlockSpec((1, k...]
    unnamed x3 -> x2, local copies, waits for them, and re-layouts: 1.85 us -> 0.01 us
    pallas_call x1, Pallas kernels: 97 us -> 95.3 us  [butterfly(): pl.pallas_call(functools.partial(butterfly_kernel, sizes), out_shape=jax....]
where the time goes in v2:
time: 103 us; the launch traced here: 101 us
  Pallas kernels  101 us (98%)
    pallas_call x1, Pallas kernels, butterfly(): pl.pallas_call(functools.partial(butterfly_kernel, sizes), out_shape=jax....  95.3 us
    pallas_call x1, Pallas kernels, expand(): pl.pallas_call(expand_kernel, grid=(nodes,), in_specs=[pl.BlockSpec((1, k...  5.75 us

profile of v2, /device:TPU:1, one launch (start us, length us, event | category | flops | bytes accessed | tf_op | source)
XLA Modules:
  0.0 101.1 jit_solution(17972450396560637186)
XLA Ops:
  0.0 0.0 copy-start
  0.0 95.3 %shard_map.46.c_ref = f32[2,192,1024]{2,1,0:T(8,128)S(1)} custom-call(f32[2,1024,1024]{2,1,0:T(8,128)} %bitcast.7, f32[2,192,1024]{2,1,0:T(8,128)} %bitcast.9, f32[6,2,2,192,192]{4,3,2,1,0:T(8,128)} %bitcast.8), custom_call_target="tpu_custom_call" | custom-call | tf_op jit(solution)/shard_map/pallas_call | solution.py:413
  95.3 0.0 copy-done
  95.3 5.8 %shard_map.47 = f32[2,1024,1024]{2,1,0:T(8,128)} custom-call(f32[2,192,1024]{2,1,0:T(8,128)S(1)} %bitcast.6, f32[2,192,1024]{2,1,0:T(8,128)S(1)} %shard_map.46.c_ref), custom_call_target="tpu_custom_call" | custom-call | tf_op jit(solution)/shard_map/pallas_call | solution.py:39
Async XLA Ops:
  0.0 95.3 %copy-start = (f32[2,1024,192]{1,2,0:T(8,128)S(1)}, f32[2,1024,192]{1,2,0:T(8,128)}, u32[]{:S(2)}) copy-start(f32[2,1024,192]{1,2,0:T(8,128)} %param.7) | copy-start | bytes 4718596

commit v3 on v2

--- a/solution.py
+++ b/solution.py
@@ -10,9 +10,9 @@
 AXES = ("gx", "gy", "gz")
 CHUNKS = 8
 ORDER = (
-    15, 0, 10, 0, 13, 0, 12, 11, 21, 1, 2, 1, 14, 1, 2, 0, 0, 3, 0, 3, 4, 20, 2, 1, 2, 1, 3, 5, 2, 0, 4, 1, 3, 6, 5, 4,
-    5, 3, 2, 1, 0, 4, 6, 2, 4, 6, 5, 5, 3, 7, 1, 6, 2, 7, 3, 4, 6, 5, 7, 4, 3, 8, 6, 5, 7, 8, 4, 6, 5, 7, 7, 6, 8, 8,
-    7, 8, 8, 7, 8, 8,
+    15, 13, 0, 0, 12, 21, 0, 14, 11, 10, 1, 0, 1, 2, 2, 1, 3, 2, 0, 0, 3, 20, 4, 3, 1, 2, 1, 5, 0, 4, 2, 1, 3, 5, 6, 4,
+    2, 5, 4, 3, 1, 0, 6, 3, 6, 4, 5, 2, 1, 5, 4, 7, 7, 6, 2, 3, 5, 7, 6, 4, 3, 6, 5, 7, 4, 6, 5, 7, 8, 6, 8, 7,
+    8, 7, 8, 8, 7, 8, 8, 8,
 )
 
 

time: 103 us -> 101 us (0.981); the launches traced: 101 us -> 100 us
  no operation moved by 1% of the time
where the time goes in v3:
time: 101 us; the launch traced here: 100 us
  Pallas kernels  100 us (99%)
    pallas_call x1, Pallas kernels, butterfly(): pl.pallas_call(functools.partial(butterfly_kernel, sizes), out_shape=jax....  94.5 us
    pallas_call x1, Pallas kernels, expand(): pl.pallas_call(expand_kernel, grid=(nodes,), in_specs=[pl.BlockSpec((1, k...  5.75 us

profile of v3, /device:TPU:1, one launch (start us, length us, event | category | flops | bytes accessed | tf_op | source)
XLA Modules:
  0.0 100.2 jit_solution(11431304694110698062)
XLA Ops:
  0.0 0.0 copy-start
  0.0 94.5 %shard_map.46.c_ref = f32[2,192,1024]{2,1,0:T(8,128)S(1)} custom-call(f32[2,1024,1024]{2,1,0:T(8,128)} %bitcast.7, f32[2,192,1024]{2,1,0:T(8,128)} %bitcast.9, f32[6,2,2,192,192]{4,3,2,1,0:T(8,128)} %bitcast.8), custom_call_target="tpu_custom_call" | custom-call | tf_op jit(solution)/shard_map/pallas_call | solution.py:413
  94.5 0.0 copy-done
  94.5 5.8 %shard_map.47 = f32[2,1024,1024]{2,1,0:T(8,128)} custom-call(f32[2,192,1024]{2,1,0:T(8,128)S(1)} %bitcast.6, f32[2,192,1024]{2,1,0:T(8,128)S(1)} %shard_map.46.c_ref), custom_call_target="tpu_custom_call" | custom-call | tf_op jit(solution)/shard_map/pallas_call | solution.py:39
Async XLA Ops:
  0.0 94.5 %copy-start = (f32[2,1024,192]{1,2,0:T(8,128)S(1)}, f32[2,1024,192]{1,2,0:T(8,128)}, u32[]{:S(2)}) copy-start(f32[2,1024,192]{1,2,0:T(8,128)} %param.7) | copy-start | bytes 4718596

commit v4 on v3

--- a/solution.py
+++ b/solution.py
@@ -315,7 +315,10 @@
 
     def mixed(level, index, one, other):
         pair = [jnp.concatenate([a, b], axis=0) for a, b in zip(one, other)]
-        return product((w_hi[level, index], w_lo[level, index]), pair)
+        high = w_hi[level, index]
+        weight = jnp.concatenate([high, high, w_lo[level, index]], axis=1)
+        stacked = jnp.concatenate([pair[0], pair[1], pair[0]], axis=0)
+        return jnp.dot(weight, stacked, preferred_element_type=jnp.float32)
 
     def task(s, c):
         if s == 0:

time: 101 us -> 101 us (level)
  no operation moved by 1% of the time
where the time goes in v4:
time: 101 us; the launch traced here: 100 us
  Pallas kernels  100 us (99%)
    pallas_call x1, Pallas kernels, butterfly(): pl.pallas_call(functools.partial(butterfly_kernel, sizes), out_shape=jax....  94.6 us
    pallas_call x1, Pallas kernels, expand(): pl.pallas_call(expand_kernel, grid=(nodes,), in_specs=[pl.BlockSpec((1, k...  5.75 us

profile of v4, /device:TPU:1, one launch (start us, length us, event | category | flops | bytes accessed | tf_op | source)
XLA Modules:
  0.0 100.4 jit_solution(14312060974874495457)
XLA Ops:
  0.0 0.0 copy-start
  0.0 94.6 %shard_map.46.c_ref = f32[2,192,1024]{2,1,0:T(8,128)S(1)} custom-call(f32[2,1024,1024]{2,1,0:T(8,128)} %bitcast.7, f32[2,192,1024]{2,1,0:T(8,128)} %bitcast.9, f32[6,2,2,192,192]{4,3,2,1,0:T(8,128)} %bitcast.8), custom_call_target="tpu_custom_call" | custom-call | tf_op jit(solution)/shard_map/pallas_call | solution.py:416
  94.6 0.0 copy-done
  94.6 5.7 %shard_map.47 = f32[2,1024,1024]{2,1,0:T(8,128)} custom-call(f32[2,192,1024]{2,1,0:T(8,128)S(1)} %bitcast.6, f32[2,192,1024]{2,1,0:T(8,128)S(1)} %shard_map.46.c_ref), custom_call_target="tpu_custom_call" | custom-call | tf_op jit(solution)/shard_map/pallas_call | solution.py:39
Async XLA Ops:
  0.0 94.6 %copy-start = (f32[2,1024,192]{1,2,0:T(8,128)S(1)}, f32[2,1024,192]{1,2,0:T(8,128)}, u32[]{:S(2)}) copy-start(f32[2,1024,192]{1,2,0:T(8,128)} %param.7) | copy-start | bytes 4718596
